TPU v7x, 32 devices: a whole 2x2x4 slice. The times are simulated.
32 devices in a mesh: row: 4 (over y, x), col: 8 (over z, core).
Axes of the slice: x: 2, y: 2, z: 4, core: 2. Of those that a mesh axis runs over, the one named last changes fastest.
Arguments:
- node_features: bfloat16 [2048, 128, 512], P(('row', 'col')), may hold values from -6 to 6
- node_counts: int32 [2048], P(('row', 'col')), may hold values from 16 to 128, as said below
- edge_list: int32 [2048, 2, 256], P(('row', 'col')), may hold values from 0 to 128, as said below
- readout_ids: int32 [2048], P(('row', 'col')), may hold values from 0 to 255
- live_graphs: int32 [32], P(('row', 'col')), may hold values from 1 to 64, as said below
- self_weight: float32 [1], replicated, may hold values from 0.5 to 1.5
- w_first: bfloat16 [512, 512], replicated, may hold values from -0.25 to 0.25
- b_first: float32 [512], replicated, may hold values from -3 to 3
- w_second: bfloat16 [512, 512], replicated, may hold values from -0.25 to 0.25
- b_second: float32 [512], replicated, may hold values from -3 to 3
- w_third: bfloat16 [512, 512], replicated, may hold values from -0.25 to 0.25
- b_third: float32 [512], replicated, may hold values from -3 to 3
Outputs:
- node_out: bfloat16 [1024, 128, 512], P(('row', 'col'))
- readout: float32 [256, 512], P(('row', 'col'))
Inputs may be any that keep to these rules, and one draw needn't show every extreme that they name: `live_graphs`: the entries sum to 1024, and at least one equals 64. `node_counts`: node slots 0 to count - 1 of a graph are live; the rest of its block is padding. `edge_list`: each edge slot holds two node indices below its graph's node count, or 128 in both rows for an unused slot.
All inputs are finite; a program needn't handle non-finite values.
Results may differ from a plain program's by a relative error of at most 0.0058.
Values may be sent and summed in bfloat16 or wider, within the bound.
A program may use at most 128 MiB of HBM per device.

v0:
```python
import jax
import jax.numpy as jnp
from jax import lax
from jax.sharding import PartitionSpec as P

G_DEV = 32
READ_DEV = 8


def blend_nodes(features, edge_slots, self_weight):
    node_index = lax.broadcasted_iota(jnp.int32, (1, 1, features.shape[1]), 2)
    sources = (edge_slots[:, 0, :, None] == node_index).astype(jnp.bfloat16)
    targets = (edge_slots[:, 1, :, None] == node_index).astype(jnp.bfloat16)
    adjacency = jnp.einsum(
        "gek,gel->gkl", targets, sources, preferred_element_type=jnp.float32
    ).astype(jnp.bfloat16)
    neighbour = jnp.einsum("gkl,glh->gkh", adjacency, features, preferred_element_type=jnp.float32)
    return (self_weight[0] * features.astype(jnp.float32) + neighbour).astype(jnp.bfloat16)


def perceptron(blended, weights):
    w_first, b_first, w_second, b_second, w_third, b_third = weights
    flat_rows = blended.reshape(-1, blended.shape[-1])
    hidden_one = jax.nn.relu(
        jnp.dot(flat_rows, w_first, preferred_element_type=jnp.float32) + b_first
    ).astype(jnp.bfloat16)
    hidden_two = jax.nn.relu(
        jnp.dot(hidden_one, w_second, preferred_element_type=jnp.float32) + b_second
    ).astype(jnp.bfloat16)
    result = jnp.dot(hidden_two, w_third, preferred_element_type=jnp.float32) + b_third
    return result.reshape(blended.shape)


def arrival_index(slot_tags):
    wanted = lax.broadcasted_iota(jnp.int32, (G_DEV, slot_tags.shape[0]), 0)
    places = lax.broadcasted_iota(jnp.int32, (G_DEV, slot_tags.shape[0]), 1)
    return jnp.sum(jnp.where(slot_tags[None, :] == wanted, places, 0), axis=1)


def readout_terms(graph_ids, pooled, row_count):
    id_keys = lax.broadcasted_iota(jnp.int32, (row_count, graph_ids.shape[0]), 0)
    members = (id_keys == graph_ids[None, :]).astype(jnp.float32)
    return jnp.dot(
        members, pooled, precision=lax.Precision.HIGHEST, preferred_element_type=jnp.float32
    )


def body(
    node_features,
    node_counts,
    edge_list,
    readout_ids,
    live_graphs,
    self_weight,
    w_first,
    b_first,
    w_second,
    b_second,
    w_third,
    b_third,
):
    weights = (w_first, b_first, w_second, b_second, w_third, b_third)
    devices = lax.axis_size(("row", "col"))
    capacity = node_features.shape[0]
    bucket = (capacity + devices - 1) // devices
    own_count = live_graphs[0]
    every_count = lax.all_gather(live_graphs, ("row", "col"), axis=0, tiled=True)
    position = lax.broadcasted_iota(jnp.int32, (devices,), 0)
    offset = jnp.sum(jnp.where(position < lax.axis_index(("row", "col")), every_count, 0))
    targets = lax.broadcasted_iota(jnp.int32, (devices * bucket,), 0)
    dest_device = targets // bucket
    within = (dest_device - offset) % devices + targets % bucket * devices
    sending_ok = within < own_count
    slot_tags = jnp.where(sending_ok, (offset + within) // devices, G_DEV)
    picked = jnp.minimum(within, capacity - 1)
    node_index = lax.broadcasted_iota(jnp.int32, (1, node_features.shape[1]), 1)
    blended = blend_nodes(node_features, edge_list, self_weight)
    live_nodes = node_index < node_counts[:, None]
    results = jnp.where(live_nodes[:, :, None], perceptron(blended, weights), 0.0).astype(
        jnp.bfloat16
    )
    pooled = jnp.sum(results.astype(jnp.float32), axis=1) / node_counts[:, None].astype(jnp.float32)
    slot_live = lax.broadcasted_iota(jnp.int32, (capacity,), 0) < own_count
    graph_ids = jnp.where(slot_live, readout_ids, -1)
    arrived, arrived_tags = (
        lax.all_to_all(results[picked], ("row", "col"), split_axis=0, concat_axis=0, tiled=True),
        lax.all_to_all(slot_tags, ("row", "col"), split_axis=0, concat_axis=0, tiled=True),
    )
    node_out = arrived[arrival_index(arrived_tags)]
    totals = lax.psum(readout_terms(graph_ids, pooled, READ_DEV * devices), ("row", "col"))
    readout = lax.dynamic_slice_in_dim(
        totals, lax.axis_index(("row", "col")) * READ_DEV, READ_DEV, 0
    )
    return (node_out, readout)


def solution(mesh):
    in_specs = (
        P(("row", "col"), None, None),
        P(("row", "col")),
        P(("row", "col"), None, None),
        P(("row", "col")),
        P(("row", "col")),
        P(),
        P(),
        P(),
        P(),
        P(),
        P(),
        P(),
    )
    out_specs = (P(("row", "col"), None, None), P(("row", "col"), None))
    return jax.shard_map(body, mesh=mesh, in_specs=in_specs, out_specs=out_specs, check_vma=False)
```

profile of v0, /device:TPU:0, one launch (start us, length us, event | category | flops | bytes accessed | tf_op | source)
XLA Modules:
  0.0 323.4 jit_solution(11251081128402884339)
XLA Ops:
  7.2 0.0 copy-start
  7.9 0.1 dynamic-update-slice
  8.0 41.9 %all-reduce = s32[32]{0:T(128)S(1)} all-reduce(s32[32]{0:T(128)S(1)} %dynamic-update-slice), channel_id=1, replica_groups=mesh['row'=4,'col'=8] {'row','col'}, use_global_device_ids=true, to_apply=%add | all-reduce | flops 32 | bytes 256
  50.0 0.6 fusion.15
  50.6 1.4 compare_select_fusion.2
  52.0 4.4 %all-to-all-start.1 = ((s32[32,2,1]{1,2,0:T(1,128)}), s32[32,2,1]{1,2,0:T(1,128)S(1)}, u32[]{:S(2)}, u32[]{:S(2)}) async-start(s32[32,2,1]{1,2,0:T(1,128)} %compare_select_fusion.2), calls=%async_computation.1 | async-start | bytes 32768 | tf_op jit(solution)/shard_map/all_to_all | solution.py:87
  56.4 0.7 fusion.17
  57.1 1.1 fusion.20
  58.8 0.7 iota_compare_fusion.14
  59.6 0.0 copy-start.4
  59.6 12.6 %add_convert_fusion = bf16[64,128,512]{2,1,0:T(8,128)(2,1)} fusion(bf16[64,128,512]{2,1,0:T(8,128)(2,1)} %param.12, f32[]{:T(128)} %bitcast.24, s32[64,256]{1,0:T(8,128)S(1)} %get-tuple-element.6, s32[64,256]{1,0:T(8,128)S(1)} %get-tuple-element.7), kind=kOutput, calls=%fused_computation.6 | convolution fusion | flops 1632632832 | bytes 16908292 | tf_op jit(solution)/shard_map/gkl,glh->gkh/dot_general | solution.py:17
  72.2 0.0 copy-start.3
  72.2 0.0 copy-start.5
  72.2 0.0 copy-start.6
  72.2 10.2 %maximum_convert_fusion.1 = bf16[8192,512]{1,0:T(8,128)(2,1)} fusion(bf16[8192,512]{1,0:T(8,128)(2,1)} %bitcast.25, bf16[512,512]{1,0:T(8,128)(2,1)S(1)} %copy-done, f32[512]{0:T(512)S(1)} %copy-done.4), kind=kOutput, calls=%fused_computation.5 | convolution fusion | flops 4307550208 | bytes 17303552 | tf_op jit(solution)/shard_map/dot_general | solution.py:25
  82.4 0.0 copy-done.3
  82.5 13.3 %convolution_add_fusion = bf16[8192,512]{1,0:T(8,128)(2,1)} fusion(bf16[512,512]{1,0:T(8,128)(2,1)S(1)} %copy-done.2, f32[512]{0:T(512)S(1)} %copy-done.5, bf16[8192,512]{1,0:T(8,128)(2,1)} %maximum_convert_fusion.1, bf16[512,512]{1,0:T(8,128)(2,1)S(1)} %copy-done.3, f32[512]{0:T(512)S(1)} %copy-done.6), kind=kOutput, calls=%fused_computation.7 | convolution fusion | flops 8610906112 | bytes 17829888 | tf_op jit(solution)/shard_map/dot_general | solution.py:30
  95.7 8.3 %convert_reduce_fusion = (f32[64,512]{1,0:T(8,128)S(1)}, bf16[64,128,512]{2,1,0:T(8,128)(2,1)}) fusion(pred[64,128]{1,0:T(8,128)(4,1)S(1)} %iota_compare_fusion.14, bf16[8192,512]{1,0:T(8,128)(2,1)} %convolution_add_fusion), kind=kLoop, calls=%fused_computation.2 | loop fusion | flops 12550144 | bytes 16916480 | tf_op jit(solution)/shard_map/reduce_sum | solution.py:82
  104.1 8.9 %gather_fusion = bf16[64,128,512]{2,1,0:T(8,128)(2,1)} fusion(bf16[64,128,512]{2,1,0:T(8,128)(2,1)} %get-tuple-element.3, s32[1024]{0:T(1024)S(1)} %pad_clamp_fusion.1), kind=kCustom, calls=%fused_computation | custom fusion | bytes 16777472 | tf_op jit(solution)/shard_map/gather | solution.py:86
  113.0 0.0 all-to-all-done.1
  113.0 6.0 %all-to-all-start = ((bf16[64,128,512]{2,1,0:T(8,128)(2,1)}), bf16[64,128,512]{2,1,0:T(8,128)(2,1)}, u32[]{:S(2)}, u32[]{:S(2)}) async-start(bf16[64,128,512]{2,1,0:T(8,128)(2,1)} %gather_fusion), calls=%async_computation | async-start | bytes 16777216 | tf_op jit(solution)/shard_map/all_to_all | solution.py:86
  119.0 0.0 all-reduce.3.cloned.1.call-start
  119.0 1.2 fusion.4
  120.3 0.0 all-reduce.3.cloned.1.call-update
  120.3 0.5 broadcast.399
  120.8 0.7 reduce.3
  121.5 0.1 eq.59
  121.6 0.1 select_reduce_fusion
  121.8 173.9 %all-reduce.3.cloned.1.call-done = f32[256,512]{1,0:T(8,128)} async-done(((f32[256,512]{1,0:T(8,128)}), f32[256,512]{1,0:T(8,128)}) %all-reduce.3.cloned.1.call-update) | async-done | bytes 524304 | tf_op jit(solution)/shard_map/psum | solution.py:90
  295.6 1.3 constant_dynamic-slice_fusion
  297.0 13.4 %all-to-all-done = bf16[64,128,512]{2,1,0:T(8,128)(2,1)} async-done(((bf16[64,128,512]{2,1,0:T(8,128)(2,1)}), bf16[64,128,512]{2,1,0:T(8,128)(2,1)}, u32[]{:S(2)}, u32[]{:S(2)}) %all-to-all-start) | async-done | bytes 8388640 | tf_op jit(solution)/shard_map/all_to_all | solution.py:86
  310.4 6.2 %gather_fusion.1 = bf16[32,128,512]{2,1,0:T(8,128)(2,1)} fusion(bf16[64,128,512]{2,1,0:T(8,128)(2,1)} %all-to-all-done, s32[1024]{0:T(1024)S(1)} %pad_clamp_fusion), kind=kCustom, calls=%fused_computation.1 | custom fusion | bytes 8388736 | tf_op jit(solution)/shard_map/gather | solution.py:89
  (17 shorter events, 0.1 us)
Async XLA Ops:
  7.2 65.0 %copy-start = (bf16[512,512]{1,0:T(8,128)(2,1)S(1)}, bf16[512,512]{1,0:T(8,128)(2,1)}, u32[]{:S(2)}) copy-start(bf16[512,512]{1,0:T(8,128)(2,1)} %param.18) | copy-start | bytes 1572868
  52.0 61.0 %all-to-all-start.1 = ((s32[32,2,1]{1,2,0:T(1,128)}), s32[32,2,1]{1,2,0:T(1,128)S(1)}, u32[]{:S(2)}, u32[]{:S(2)}) async-start(s32[32,2,1]{1,2,0:T(1,128)} %compare_select_fusion.2), calls=%async_computation.1 | async-start | bytes 32768 | tf_op jit(solution)/shard_map/all_to_all | solution.py:87
  59.6 12.6 %copy-start.4 = (f32[512]{0:T(512)S(1)}, f32[512]{0:T(512)}, u32[]{:S(2)}) copy-start(f32[512]{0:T(512)} %param.19) | copy-start | bytes 6148
  72.2 10.3 %copy-start.2 = (bf16[512,512]{1,0:T(8,128)(2,1)S(1)}, bf16[512,512]{1,0:T(8,128)(2,1)}, u32[]{:S(2)}) copy-start(bf16[512,512]{1,0:T(8,128)(2,1)} %param.22) | copy-start | bytes 1572868
  72.2 10.3 %copy-start.3 = (bf16[512,512]{1,0:T(8,128)(2,1)S(1)}, bf16[512,512]{1,0:T(8,128)(2,1)}, u32[]{:S(2)}) copy-start(bf16[512,512]{1,0:T(8,128)(2,1)} %param.20) | copy-start | bytes 1572868
  72.2 10.3 %copy-start.5 = (f32[512]{0:T(512)S(1)}, f32[512]{0:T(512)}, u32[]{:S(2)}) copy-start(f32[512]{0:T(512)} %param.23) | copy-start | bytes 6148
  72.2 10.3 %copy-start.6 = (f32[512]{0:T(512)S(1)}, f32[512]{0:T(512)}, u32[]{:S(2)}) copy-start(f32[512]{0:T(512)} %param.21) | copy-start | bytes 6148
  113.0 6.0 %copy-start.1 = (s32[64]{0:T(128)S(1)}, s32[64]{0:T(128)}, u32[]{:S(2)}) copy-start(s32[64]{0:T(128)} %param.13) | copy-start | bytes 772
  113.0 6.1 %copy-start.7 = (s32[64]{0:T(128)S(1)}, s32[64]{0:T(128)}, u32[]{:S(2)}) copy-start(s32[64]{0:T(128)} %param.15) | copy-start | bytes 772
  113.0 197.4 %all-to-all-start = ((bf16[64,128,512]{2,1,0:T(8,128)(2,1)}), bf16[64,128,512]{2,1,0:T(8,128)(2,1)}, u32[]{:S(2)}, u32[]{:S(2)}) async-start(bf16[64,128,512]{2,1,0:T(8,128)(2,1)} %gather_fusion), calls=%async_computation | async-start | bytes 16777216 | tf_op jit(solution)/shard_map/all_to_all | solution.py:86
  119.0 176.7 %all-reduce.3.cloned.1.call-start = ((), (), s32[]{:S(2)}) async-start(), calls=%async_computation.2 | async-start | bytes 1048576 | tf_op jit(solution)/shard_map/psum | solution.py:90
Sparse Core Ops, SparseCore 0:
  125.6 169.9 all-reduce.2
where the time goes:
time: 324 us; the launch traced here: 323 us
  waiting for transfers between devices  187 us (58%)
  blocking collectives  41.9 us (13%)
  matrix products  37.3 us (12%)
  local copies, waits for them, and re-layouts  18.3 us (6%)
  between operations  15.6 us (5%)
  other arithmetic  12.6 us (4%)
  starting transfers between devices  10.4 us (3%)
    psum x1, waiting for transfers between devices, body(): lax.psum(readout_terms(graph_ids, pooled, READ_DEV * devices), ('row', 'c...  174 us
    unnamed x1, blocking collectives  41.9 us
    all_to_all x1, waiting for transfers between devices, body(): lax.all_to_all(results[picked], ('row', 'col'), split_axis=0, concat_axis...  13.4 us
    dot_general x1, matrix products, perceptron(): jnp.dot(hidden_two, w_third, preferred_element_type=jnp.float32) + b_third  13.3 us
    dot_general x1, matrix products, blend_nodes(): jnp.einsum('gkl,glh->gkh', adjacency, features, preferred_element_type=jn...  12.6 us
    dot_general x1, matrix products, perceptron(): jnp.dot(flat_rows, w_first, preferred_element_type=jnp.float32) + b_first  10.2 us
    gather x1, local copies, waits for them, and re-layouts, body(): results[picked]  8.91 us
    reduce_sum x1, other arithmetic, body(): jnp.sum(results.astype(jnp.float32), axis=1)  8.33 us
  transfers between devices with their start and end apart: 3, of which 2 were waited for; matrix products, arithmetic and copies ran while one was open for 18% of the time, Pallas kernels for 0%

commit v1 on v0

--- a/solution.py
+++ b/solution.py
@@ -87,7 +87,9 @@
         lax.all_to_all(slot_tags, ("row", "col"), split_axis=0, concat_axis=0, tiled=True),
     )
     node_out = arrived[arrival_index(arrived_tags)]
-    totals = lax.psum(readout_terms(graph_ids, pooled, READ_DEV * devices), ("row", "col"))
+    totals = jnp.sum(
+        lax.all_gather(readout_terms(graph_ids, pooled, READ_DEV * devices), ("row", "col")), axis=0
+    )
     readout = lax.dynamic_slice_in_dim(
         totals, lax.axis_index(("row", "col")) * READ_DEV, READ_DEV, 0
     )

time: 324 us -> 374 us (1.15)
  waiting for transfers between devices: 187 us -> 228 us
  other arithmetic: 12.6 us -> 20.9 us
    all_to_all x1, waiting for transfers between devices: 13.4 us -> 228 us  [body(): lax.all_to_all(results[picked], ('row', 'col'), split_axis=0, concat_axis...]
    psum x1 -> x0, waiting for transfers between devices: 174 us -> none  [body(): lax.psum(readout_terms(graph_ids, pooled, READ_DEV * devices), ('row', 'c...]
    reduce_sum x0 -> x1, other arithmetic: none -> 7.81 us  [body(): jnp.sum(lax.all_gather(readout_terms(graph_ids, pooled, READ_DEV * device...]
  transfers between devices with their start and end apart: 3 -> 3, of which waited for: 2 -> 1; matrix products, arithmetic and copies ran while one was open for 18% -> 5% of each run, Pallas kernels for 0% -> 0%
where the time goes in v1:
time: 374 us; the launch traced here: 373 us
  waiting for transfers between devices  228 us (61%)
  blocking collectives  43.6 us (12%)
  matrix products  37.3 us (10%)
  other arithmetic  20.9 us (6%)
  local copies, waits for them, and re-layouts  17.7 us (5%)
  between operations  15.5 us (4%)
  starting transfers between devices  10.2 us (3%)
    all_to_all x1, waiting for transfers between devices, body(): lax.all_to_all(results[picked], ('row', 'col'), split_axis=0, concat_axis...  228 us
    unnamed x1, blocking collectives  43.6 us
    dot_general x1, matrix products, perceptron(): jnp.dot(hidden_two, w_third, preferred_element_type=jnp.float32) + b_third  13.3 us
    dot_general x1, matrix products, blend_nodes(): jnp.einsum('gkl,glh->gkh', adjacency, features, preferred_element_type=jn...  12.6 us
    dot_general x1, matrix products, perceptron(): jnp.dot(flat_rows, w_first, preferred_element_type=jnp.float32) + b_first  10.2 us
    gather x1, local copies, waits for them, and re-layouts, body(): results[picked]  9.01 us
    reduce_sum x1, other arithmetic, body(): jnp.sum(results.astype(jnp.float32), axis=1)  8.32 us
    reduce_sum x1, other arithmetic, body(): jnp.sum(lax.all_gather(readout_terms(graph_ids, pooled, READ_DEV * device...  7.81 us
  transfers between devices with their start and end apart: 3, of which 1 were waited for; matrix products, arithmetic and copies ran while one was open for 5% of the time, Pallas kernels for 0%

profile of v1, /device:TPU:0, one launch (start us, length us, event | category | flops | bytes accessed | tf_op | source)
XLA Modules:
  0.0 373.4 jit_solution(9964921495333553476)
XLA Ops:
  7.2 0.0 copy-start
  7.2 0.0 all-gather.3.cloned.1.call-start
  7.2 0.8 iota_compare_fusion.14
  8.0 0.7 convert_element_type.35
  9.3 1.1 fusion.20
  11.1 0.0 copy-start.4
  11.1 12.6 %add_convert_fusion = bf16[64,128,512]{2,1,0:T(8,128)(2,1)} fusion(bf16[64,128,512]{2,1,0:T(8,128)(2,1)} %param.12, f32[]{:T(128)} %bitcast.25, s32[64,256]{1,0:T(8,128)S(1)} %get-tuple-element.6, s32[64,256]{1,0:T(8,128)S(1)} %get-tuple-element.7), kind=kOutput, calls=%fused_computation.6 | convolution fusion | flops 1632632832 | bytes 16908292 | tf_op jit(solution)/shard_map/gkl,glh->gkh/dot_general | solution.py:17
  23.7 0.0 copy-start.3
  23.7 0.0 copy-start.5
  23.7 0.0 copy-start.6
  23.7 10.2 %maximum_convert_fusion.1 = bf16[8192,512]{1,0:T(8,128)(2,1)} fusion(bf16[8192,512]{1,0:T(8,128)(2,1)} %bitcast.27, bf16[512,512]{1,0:T(8,128)(2,1)S(1)} %copy-done, f32[512]{0:T(512)S(1)} %copy-done.4), kind=kOutput, calls=%fused_computation.5 | convolution fusion | flops 4307550208 | bytes 17303552 | tf_op jit(solution)/shard_map/dot_general | solution.py:25
  34.0 13.3 %convolution_add_fusion = bf16[8192,512]{1,0:T(8,128)(2,1)} fusion(bf16[512,512]{1,0:T(8,128)(2,1)S(1)} %copy-done.2, f32[512]{0:T(512)S(1)} %copy-done.5, bf16[8192,512]{1,0:T(8,128)(2,1)} %maximum_convert_fusion.1, bf16[512,512]{1,0:T(8,128)(2,1)S(1)} %copy-done.3, f32[512]{0:T(512)S(1)} %copy-done.6), kind=kOutput, calls=%fused_computation.7 | convolution fusion | flops 8610906112 | bytes 17829888 | tf_op jit(solution)/shard_map/dot_general | solution.py:30
  47.3 8.3 %convert_reduce_fusion = (f32[64,512]{1,0:T(8,128)S(1)}, bf16[64,128,512]{2,1,0:T(8,128)(2,1)}) fusion(pred[64,128]{1,0:T(8,128)(4,1)S(1)} %iota_compare_fusion.14, bf16[8192,512]{1,0:T(8,128)(2,1)} %convolution_add_fusion), kind=kLoop, calls=%fused_computation.2 | loop fusion | flops 12550144 | bytes 16916480 | tf_op jit(solution)/shard_map/reduce_sum | solution.py:82
  55.6 1.3 fusion.4
  56.8 0.0 all-gather.3.cloned.1.call-update
  56.9 0.1 dynamic-update-slice
  57.0 43.6 %all-reduce = s32[32]{0:T(128)S(1)} all-reduce(s32[32]{0:T(128)S(1)} %dynamic-update-slice), channel_id=1, replica_groups=mesh['row'=4,'col'=8] {'row','col'}, use_global_device_ids=true, to_apply=%add | all-reduce | flops 32 | bytes 256
  100.6 0.6 fusion.15
  101.3 1.3 compare_select_fusion.2
  102.6 4.5 %all-to-all-start.1 = ((s32[32,2,1]{1,2,0:T(1,128)}), s32[32,2,1]{1,2,0:T(1,128)S(1)}, u32[]{:S(2)}, u32[]{:S(2)}) async-start(s32[32,2,1]{1,2,0:T(1,128)} %compare_select_fusion.2), calls=%async_computation.1 | async-start | bytes 32768 | tf_op jit(solution)/shard_map/all_to_all | solution.py:87
  107.1 0.6 fusion.17
  107.7 9.0 %gather_fusion = bf16[64,128,512]{2,1,0:T(8,128)(2,1)} fusion(bf16[64,128,512]{2,1,0:T(8,128)(2,1)} %get-tuple-element.3, s32[1024]{0:T(1024)S(1)} %pad_clamp_fusion.1), kind=kCustom, calls=%fused_computation | custom fusion | bytes 16777472 | tf_op jit(solution)/shard_map/gather | solution.py:86
  116.7 0.0 all-to-all-done.1
  116.7 5.7 %all-to-all-start = ((bf16[64,128,512]{2,1,0:T(8,128)(2,1)}), bf16[64,128,512]{2,1,0:T(8,128)(2,1)}, u32[]{:S(2)}, u32[]{:S(2)}) async-start(bf16[64,128,512]{2,1,0:T(8,128)(2,1)} %gather_fusion), calls=%async_computation | async-start | bytes 16777216 | tf_op jit(solution)/shard_map/all_to_all | solution.py:86
  122.4 0.5 broadcast.399
  122.9 0.7 reduce.3
  123.6 0.1 eq.59
  123.7 0.1 select_reduce_fusion
  123.9 228.0 %all-to-all-done = bf16[64,128,512]{2,1,0:T(8,128)(2,1)} async-done(((bf16[64,128,512]{2,1,0:T(8,128)(2,1)}), bf16[64,128,512]{2,1,0:T(8,128)(2,1)}, u32[]{:S(2)}, u32[]{:S(2)}) %all-to-all-start) | async-done | bytes 8388640 | tf_op jit(solution)/shard_map/all_to_all | solution.py:86
  351.9 6.2 %gather_fusion.1 = bf16[32,128,512]{2,1,0:T(8,128)(2,1)} fusion(bf16[64,128,512]{2,1,0:T(8,128)(2,1)} %all-to-all-done, s32[1024]{0:T(1024)S(1)} %pad_clamp_fusion), kind=kCustom, calls=%fused_computation.1 | custom fusion | bytes 8388736 | tf_op jit(solution)/shard_map/gather | solution.py:89
  358.1 7.8 %reduce_sum.42 = f32[256,512]{1,0:T(8,128)S(1)} reduce(f32[32,256,512]{2,1,0:T(8,128)} %bitcast.26, f32[]{:T(128)} %constant.74.clone.1), dimensions={0}, to_apply=%region_3.4 | reduce | flops 4063232 | bytes 17301508 | tf_op jit(solution)/shard_map/reduce_sum | solution.py:90
  365.9 0.6 constant_dynamic-slice_fusion
  (18 shorter events, 0.1 us)
Async XLA Ops:
  7.2 16.5 %copy-start = (bf16[512,512]{1,0:T(8,128)(2,1)S(1)}, bf16[512,512]{1,0:T(8,128)(2,1)}, u32[]{:S(2)}) copy-start(bf16[512,512]{1,0:T(8,128)(2,1)} %param.18) | copy-start | bytes 1572868
  7.2 350.9 %all-gather.3.cloned.1.call-start = ((), (), s32[]{:S(2)}) async-start(), calls=%async_computation.2 | async-start | bytes 17301504 | tf_op jit(solution)/shard_map/all_gather | solution.py:91
  11.1 12.6 %copy-start.4 = (f32[512]{0:T(512)S(1)}, f32[512]{0:T(512)}, u32[]{:S(2)}) copy-start(f32[512]{0:T(512)} %param.19) | copy-start | bytes 6148
  23.7 10.3 %copy-start.2 = (bf16[512,512]{1,0:T(8,128)(2,1)S(1)}, bf16[512,512]{1,0:T(8,128)(2,1)}, u32[]{:S(2)}) copy-start(bf16[512,512]{1,0:T(8,128)(2,1)} %param.22) | copy-start | bytes 1572868
  23.7 10.3 %copy-start.3 = (bf16[512,512]{1,0:T(8,128)(2,1)S(1)}, bf16[512,512]{1,0:T(8,128)(2,1)}, u32[]{:S(2)}) copy-start(bf16[512,512]{1,0:T(8,128)(2,1)} %param.20) | copy-start | bytes 1572868
  23.7 10.3 %copy-start.5 = (f32[512]{0:T(512)S(1)}, f32[512]{0:T(512)}, u32[]{:S(2)}) copy-start(f32[512]{0:T(512)} %param.23) | copy-start | bytes 6148
  23.7 10.3 %copy-start.6 = (f32[512]{0:T(512)S(1)}, f32[512]{0:T(512)}, u32[]{:S(2)}) copy-start(f32[512]{0:T(512)} %param.21) | copy-start | bytes 6148
  47.3 8.3 %copy-start.7 = (s32[64]{0:T(128)S(1)}, s32[64]{0:T(128)}, u32[]{:S(2)}) copy-start(s32[64]{0:T(128)} %param.15) | copy-start | bytes 772
  102.6 14.1 %all-to-all-start.1 = ((s32[32,2,1]{1,2,0:T(1,128)}), s32[32,2,1]{1,2,0:T(1,128)S(1)}, u32[]{:S(2)}, u32[]{:S(2)}) async-start(s32[32,2,1]{1,2,0:T(1,128)} %compare_select_fusion.2), calls=%async_computation.1 | async-start | bytes 32768 | tf_op jit(solution)/shard_map/all_to_all | solution.py:87
  116.7 235.2 %all-to-all-start = ((bf16[64,128,512]{2,1,0:T(8,128)(2,1)}), bf16[64,128,512]{2,1,0:T(8,128)(2,1)}, u32[]{:S(2)}, u32[]{:S(2)}) async-start(bf16[64,128,512]{2,1,0:T(8,128)(2,1)} %gather_fusion), calls=%async_computation | async-start | bytes 16777216 | tf_op jit(solution)/shard_map/all_to_all | solution.py:86
  358.1 8.4 %copy-start.1 = (bf16[512,512]{1,0:T(8,128)(2,1)S(1)}, bf16[512,512]{1,0:T(8,128)(2,1)}, u32[]{:S(2)}) copy-start(bf16[512,512]{1,0:T(8,128)(2,1)} %param.18) | copy-start | bytes 1572868
Sparse Core Ops, SparseCore 0:
  57.0 181.3 all-gather.2
